TPU v7x, 256 devices: a whole 4x4x8 slice. The times are simulated.
256 devices in a mesh: cells: 16 (over z, core), lev: 16 (over x, y).
Axes of the slice: x: 4, y: 4, z: 8, core: 2. Of those that a mesh axis runs over, the one named last changes fastest.
Arguments:
- source_levels: float32 [128, 65536], P('lev', 'cells'), may hold values from -6 to 6
- level_to_mode: float32 [128, 128], replicated, may hold values from -0.5 to 0.5
- mode_to_level: float32 [128, 128], replicated, may hold values from -0.5 to 0.5
- mode_shift: float32 [128], P('lev'), may hold values from 0.02 to 1
- edge_weight: float32 [6, 65536], P(None, 'cells'), may hold values from 0.05 to 0.5
- neighbours: int32 [6, 65536], P(None, 'cells'), may hold values from 0 to 6143, as said below
- send_lists: int32 [16, 2048], P('cells'), may hold values from 0 to 4095, as said below
Outputs:
- correction: float32 [128, 65536], P('lev', 'cells')
Inputs may be any that keep to these rules, and one draw needn't show every extreme that they name: `neighbours`: an entry below 4096 is a cell of the same partition whose local index differs from the cell's own local index by at most 32; an entry e of partition p at or above 4096 names halo slot h = (e - 4096) % 128 from partition s = (e - 4096) // 128, with s not p and h below the number of cells that s sends to p. An unused entry names the cell itself. `send_lists`: the number of used slots from partition s to partition q differs from pair to pair: 1 to 128 for every pair of different partitions, 0 for a partition and itself; in every draw some partition receives 128 cells from every other one. Unused slots hold any cell.
All inputs are finite; a program needn't handle non-finite values.
Results may differ from a plain program's by a relative error of at most 0.00007.
Values sent between devices are 32-bit elements; how exact they have to be, the bound alone decides.
A program may use at most 64 MiB of HBM per device.

v0:
```python
import jax
import jax.numpy as jnp
from jax import lax
from jax.sharding import PartitionSpec as P

DEG = 6
HMAX = 128
SWEEPS = 2
STEPS = 4


def full_product(left, right):
    return jnp.dot(left, right, precision=lax.Precision.HIGHEST, preferred_element_type=jnp.float32)


def local(
    source_levels, level_to_mode, mode_to_level, mode_shift, edge_weight, neighbours, send_lists
):
    slab_rows = source_levels.shape[0]
    position = lax.axis_index("lev")
    send_cells = send_lists.reshape(-1)
    slot_total = send_cells.shape[0]
    diagonal = jnp.sum(edge_weight, axis=0)
    own_rows = lax.dynamic_slice_in_dim(level_to_mode, position * slab_rows, slab_rows, 0)
    mode_field = full_product(own_rows, lax.all_gather(source_levels, "lev", axis=0, tiled=True))
    shift_col = mode_shift[:, None]
    own_scale = shift_col + diagonal[None, :]

    def apply_operator(field):
        outgoing = jnp.take(field, send_cells, axis=1)
        arrived = lax.all_to_all(
            outgoing.reshape(slab_rows, -1, HMAX), "cells", split_axis=1, concat_axis=1, tiled=True
        ).reshape(slab_rows, slot_total)
        extended = jnp.concatenate([field, arrived], axis=1)
        running = own_scale * field
        for slot_number in range(DEG):
            running = running - edge_weight[slot_number][None, :] * jnp.take(
                extended, neighbours[slot_number], axis=1
            )
        return running

    radius = DEG / 2.0
    centre = shift_col + radius
    sigma_ratio = centre / radius
    answer = jnp.zeros_like(mode_field)
    remain = mode_field
    direction = jnp.zeros_like(mode_field)
    factor = 1.0 / sigma_ratio
    for sweep_index in range(SWEEPS):
        for step_index in range(STEPS):
            if step_index == 0:
                if sweep_index > 0:
                    remain = remain - apply_operator(direction)
                factor = 1.0 / sigma_ratio
                direction = remain / centre
            else:
                remain = remain - apply_operator(direction)
                newer = 1.0 / (2.0 * sigma_ratio - factor)
                direction = newer * factor * direction + 2.0 * newer / radius * remain
                factor = newer
            answer = answer + direction
    own_columns = lax.dynamic_slice_in_dim(mode_to_level, position * slab_rows, slab_rows, 1)
    return lax.psum_scatter(
        full_product(own_columns, answer), "lev", scatter_dimension=0, tiled=True
    )


def solution(mesh):
    in_specs = (
        P("lev", "cells"),
        P(),
        P(),
        P("lev"),
        P(None, "cells"),
        P(None, "cells"),
        P("cells", None),
    )
    out_specs = P("lev", "cells")
    return jax.shard_map(local, mesh=mesh, in_specs=in_specs, out_specs=out_specs, check_vma=False)
```

profile of v0, /device:TPU:1, one launch (start us, length us, event | category | flops | bytes accessed | tf_op | source)
XLA Modules:
  0.0 1055.3 jit_solution(7952593365196662498)
XLA Ops:
  21.0 41.8 %all-gather.2.cloned.1.call-done = f32[128,4096]{1,0:T(8,128)} async-done(((f32[8,4096]{1,0:T(8,128)}), f32[128,4096]{1,0:T(8,128)}) %all-gather.2.cloned.1.call-update) | async-done | bytes 2097168 | tf_op jit(solution)/shard_map/all_gather | solution.py:25
  66.1 6.4 gather_fusion
  74.5 8.5 all-to-all-start
  83.6 7.2 all-to-all-done
  93.4 15.4 %gather_fusion.6 = f32[4096,8]{1,0:T(8,128)} fusion(f32[8,6144]{0,1:T(8,128)S(1)} %copy.108, s32[4096]{0:T(1024)} %fusion.90), kind=kCustom, calls=%fused_computation.12.clone | custom fusion | bytes 278528 | tf_op jit(solution)/shard_map/jit(_take)/gather | solution.py:37
  108.8 2.8 copy.119
  111.6 14.1 %gather_fusion.5 = f32[4096,8]{1,0:T(8,128)} fusion(f32[8,6144]{0,1:T(8,128)S(1)} %copy.108, s32[4096]{0:T(1024)S(1)} %copy-done.49), kind=kCustom, calls=%fused_computation.11.clone | custom fusion | bytes 278528 | tf_op jit(solution)/shard_map/jit(_take)/gather | solution.py:37
  125.7 2.8 copy.117
  128.5 14.1 %gather_fusion.4 = f32[4096,8]{1,0:T(8,128)} fusion(f32[8,6144]{0,1:T(8,128)S(1)} %copy.108, s32[4096]{0:T(1024)S(1)} %copy-done.47), kind=kCustom, calls=%fused_computation.10.clone | custom fusion | bytes 278528 | tf_op jit(solution)/shard_map/jit(_take)/gather | solution.py:37
  145.4 14.1 %gather_fusion.3 = f32[4096,8]{1,0:T(8,128)} fusion(f32[8,6144]{0,1:T(8,128)S(1)} %copy.108, s32[4096]{0:T(1024)S(1)} %copy-done.45), kind=kCustom, calls=%fused_computation.9.clone | custom fusion | bytes 278528 | tf_op jit(solution)/shard_map/jit(_take)/gather | solution.py:37
  159.5 2.8 copy.113
  162.4 14.1 %gather_fusion.2 = f32[4096,8]{1,0:T(8,128)} fusion(f32[8,6144]{0,1:T(8,128)S(1)} %copy.108, s32[4096]{0:T(1024)S(1)} %copy-done.41), kind=kCustom, calls=%fused_computation.8.clone | custom fusion | bytes 278528 | tf_op jit(solution)/shard_map/jit(_take)/gather | solution.py:37
  179.3 14.1 %gather_fusion.1 = f32[4096,8]{1,0:T(8,128)} fusion(f32[8,6144]{0,1:T(8,128)S(1)} %copy.108, s32[4096]{0:T(1024)S(1)} %copy-done.43), kind=kCustom, calls=%fused_computation.1.clone | custom fusion | bytes 278528 | tf_op jit(solution)/shard_map/jit(_take)/gather | solution.py:37
  197.5 6.4 gather_fusion.7
  205.3 10.5 all_to_all.35
  218.4 14.1 %gather_fusion.13 = f32[4096,8]{1,0:T(8,128)} fusion(f32[8,6144]{0,1:T(8,128)S(1)} %copy.122, s32[4096]{0:T(1024)S(1)} %copy-done.51), kind=kCustom, calls=%fused_computation.18.clone | custom fusion | bytes 278528 | tf_op jit(solution)/shard_map/jit(_take)/gather | solution.py:37
  232.5 14.1 %gather_fusion.12 = f32[4096,8]{1,0:T(8,128)} fusion(f32[8,6144]{0,1:T(8,128)S(1)} %copy.122, s32[4096]{0:T(1024)S(1)} %copy-done.50), kind=kCustom, calls=%fused_computation.17.clone | custom fusion | bytes 278528 | tf_op jit(solution)/shard_map/jit(_take)/gather | solution.py:37
  246.6 14.1 %gather_fusion.11 = f32[4096,8]{1,0:T(8,128)} fusion(f32[8,6144]{0,1:T(8,128)S(1)} %copy.122, s32[4096]{0:T(1024)S(1)} %copy-done.48), kind=kCustom, calls=%fused_computation.16.clone | custom fusion | bytes 278528 | tf_op jit(solution)/shard_map/jit(_take)/gather | solution.py:37
  260.7 14.1 %gather_fusion.10 = f32[4096,8]{1,0:T(8,128)} fusion(f32[8,6144]{0,1:T(8,128)S(1)} %copy.122, s32[4096]{0:T(1024)S(1)} %copy-done.46), kind=kCustom, calls=%fused_computation.15.clone | custom fusion | bytes 278528 | tf_op jit(solution)/shard_map/jit(_take)/gather | solution.py:37
  274.8 14.1 %gather_fusion.9 = f32[4096,8]{1,0:T(8,128)} fusion(f32[8,6144]{0,1:T(8,128)S(1)} %copy.122, s32[4096]{0:T(1024)S(1)} %copy-done.42), kind=kCustom, calls=%fused_computation.14.clone | custom fusion | bytes 278528 | tf_op jit(solution)/shard_map/jit(_take)/gather | solution.py:37
  288.9 14.1 %gather_fusion.8 = f32[4096,8]{1,0:T(8,128)} fusion(f32[8,6144]{0,1:T(8,128)S(1)} %copy.122, s32[4096]{0:T(1024)S(1)} %copy-done.44), kind=kCustom, calls=%fused_computation.13.clone | custom fusion | bytes 278528 | tf_op jit(solution)/shard_map/jit(_take)/gather | solution.py:37
  314.8 6.4 gather_fusion.14
  323.2 3.6 all-to-all-start.2
  327.5 7.2 all-to-all-done.2
  337.2 15.4 %gather_fusion.20 = f32[4096,8]{1,0:T(8,128)} fusion(f32[8,6144]{0,1:T(8,128)S(1)} %copy.136, s32[4096]{0:T(1024)} %fusion.90), kind=kCustom, calls=%fused_computation.24.clone | custom fusion | bytes 278528 | tf_op jit(solution)/shard_map/jit(_take)/gather | solution.py:37
  352.6 15.4 %gather_fusion.19 = f32[4096,8]{1,0:T(8,128)} fusion(f32[8,6144]{0,1:T(8,128)S(1)} %copy.136, s32[4096]{0:T(1024)} %fusion.89), kind=kCustom, calls=%fused_computation.23.clone | custom fusion | bytes 278528 | tf_op jit(solution)/shard_map/jit(_take)/gather | solution.py:37
  368.0 15.4 %gather_fusion.18 = f32[4096,8]{1,0:T(8,128)} fusion(f32[8,6144]{0,1:T(8,128)S(1)} %copy.136, s32[4096]{0:T(1024)} %fusion.88), kind=kCustom, calls=%fused_computation.22.clone | custom fusion | bytes 278528 | tf_op jit(solution)/shard_map/jit(_take)/gather | solution.py:37
  383.5 15.4 %gather_fusion.17 = f32[4096,8]{1,0:T(8,128)} fusion(f32[8,6144]{0,1:T(8,128)S(1)} %copy.136, s32[4096]{0:T(1024)} %fusion.87), kind=kCustom, calls=%fused_computation.21.clone | custom fusion | bytes 278528 | tf_op jit(solution)/shard_map/jit(_take)/gather | solution.py:37
  398.9 15.4 %gather_fusion.16 = f32[4096,8]{1,0:T(8,128)} fusion(f32[8,6144]{0,1:T(8,128)S(1)} %copy.136, s32[4096]{0:T(1024)} %fusion.86), kind=kCustom, calls=%fused_computation.20.clone | custom fusion | bytes 278528 | tf_op jit(solution)/shard_map/jit(_take)/gather | solution.py:37
  414.3 15.4 %gather_fusion.15 = f32[4096,8]{1,0:T(8,128)} fusion(f32[8,6144]{0,1:T(8,128)S(1)} %copy.136, s32[4096]{0:T(1024)} %fusion.85), kind=kCustom, calls=%fused_computation.19.clone | custom fusion | bytes 278528 | tf_op jit(solution)/shard_map/jit(_take)/gather | solution.py:37
  443.1 7.6 gather_fusion.21
  452.6 10.4 all_to_all.36
  465.5 15.4 %gather_fusion.27 = f32[4096,8]{1,0:T(8,128)} fusion(f32[8,6144]{0,1:T(8,128)S(1)} %copy.150, s32[4096]{0:T(1024)} %fusion.90), kind=kCustom, calls=%fused_computation.30.clone | custom fusion | bytes 278528 | tf_op jit(solution)/shard_map/jit(_take)/gather | solution.py:37
  480.9 15.4 %gather_fusion.26 = f32[4096,8]{1,0:T(8,128)} fusion(f32[8,6144]{0,1:T(8,128)S(1)} %copy.150, s32[4096]{0:T(1024)} %fusion.89), kind=kCustom, calls=%fused_computation.29.clone | custom fusion | bytes 278528 | tf_op jit(solution)/shard_map/jit(_take)/gather | solution.py:37
  496.3 15.4 %gather_fusion.25 = f32[4096,8]{1,0:T(8,128)} fusion(f32[8,6144]{0,1:T(8,128)S(1)} %copy.150, s32[4096]{0:T(1024)} %fusion.88), kind=kCustom, calls=%fused_computation.28.clone | custom fusion | bytes 278528 | tf_op jit(solution)/shard_map/jit(_take)/gather | solution.py:37
  511.7 15.4 %gather_fusion.24 = f32[4096,8]{1,0:T(8,128)} fusion(f32[8,6144]{0,1:T(8,128)S(1)} %copy.150, s32[4096]{0:T(1024)} %fusion.87), kind=kCustom, calls=%fused_computation.27.clone | custom fusion | bytes 278528 | tf_op jit(solution)/shard_map/jit(_take)/gather | solution.py:37
  527.1 15.4 %gather_fusion.23 = f32[4096,8]{1,0:T(8,128)} fusion(f32[8,6144]{0,1:T(8,128)S(1)} %copy.150, s32[4096]{0:T(1024)} %fusion.86), kind=kCustom, calls=%fused_computation.26.clone | custom fusion | bytes 278528 | tf_op jit(solution)/shard_map/jit(_take)/gather | solution.py:37
  542.6 15.4 %gather_fusion.22 = f32[4096,8]{1,0:T(8,128)} fusion(f32[8,6144]{0,1:T(8,128)S(1)} %copy.150, s32[4096]{0:T(1024)} %fusion.85), kind=kCustom, calls=%fused_computation.25.clone | custom fusion | bytes 278528 | tf_op jit(solution)/shard_map/jit(_take)/gather | solution.py:37
  572.0 6.4 gather_fusion.28
  579.8 10.4 all_to_all.37
  592.7 15.4 %gather_fusion.34 = f32[4096,8]{1,0:T(8,128)} fusion(f32[8,6144]{0,1:T(8,128)S(1)} %copy.164, s32[4096]{0:T(1024)} %fusion.90), kind=kCustom, calls=%fused_computation.36.clone | custom fusion | bytes 278528 | tf_op jit(solution)/shard_map/jit(_take)/gather | solution.py:37
  608.2 15.4 %gather_fusion.33 = f32[4096,8]{1,0:T(8,128)} fusion(f32[8,6144]{0,1:T(8,128)S(1)} %copy.164, s32[4096]{0:T(1024)} %fusion.89), kind=kCustom, calls=%fused_computation.35.clone | custom fusion | bytes 278528 | tf_op jit(solution)/shard_map/jit(_take)/gather | solution.py:37
  623.6 15.4 %gather_fusion.32 = f32[4096,8]{1,0:T(8,128)} fusion(f32[8,6144]{0,1:T(8,128)S(1)} %copy.164, s32[4096]{0:T(1024)} %fusion.88), kind=kCustom, calls=%fused_computation.34.clone | custom fusion | bytes 278528 | tf_op jit(solution)/shard_map/jit(_take)/gather | solution.py:37
  639.0 15.4 %gather_fusion.31 = f32[4096,8]{1,0:T(8,128)} fusion(f32[8,6144]{0,1:T(8,128)S(1)} %copy.164, s32[4096]{0:T(1024)} %fusion.87), kind=kCustom, calls=%fused_computation.33.clone | custom fusion | bytes 278528 | tf_op jit(solution)/shard_map/jit(_take)/gather | solution.py:37
  654.4 15.4 %gather_fusion.30 = f32[4096,8]{1,0:T(8,128)} fusion(f32[8,6144]{0,1:T(8,128)S(1)} %copy.164, s32[4096]{0:T(1024)} %fusion.86), kind=kCustom, calls=%fused_computation.32.clone | custom fusion | bytes 278528 | tf_op jit(solution)/shard_map/jit(_take)/gather | solution.py:37
  669.8 15.4 %gather_fusion.29 = f32[4096,8]{1,0:T(8,128)} fusion(f32[8,6144]{0,1:T(8,128)S(1)} %copy.164, s32[4096]{0:T(1024)} %fusion.85), kind=kCustom, calls=%fused_computation.31.clone | custom fusion | bytes 278528 | tf_op jit(solution)/shard_map/jit(_take)/gather | solution.py:37
  697.1 7.6 gather_fusion.35
  706.5 10.3 all_to_all.38
  719.4 15.4 %gather_fusion.41 = f32[4096,8]{1,0:T(8,128)} fusion(f32[8,6144]{0,1:T(8,128)S(1)} %copy.178, s32[4096]{0:T(1024)} %fusion.90), kind=kCustom, calls=%fused_computation.42.clone | custom fusion | bytes 278528 | tf_op jit(solution)/shard_map/jit(_take)/gather | solution.py:37
  734.8 15.4 %gather_fusion.40 = f32[4096,8]{1,0:T(8,128)} fusion(f32[8,6144]{0,1:T(8,128)S(1)} %copy.178, s32[4096]{0:T(1024)} %fusion.89), kind=kCustom, calls=%fused_computation.41.clone | custom fusion | bytes 278528 | tf_op jit(solution)/shard_map/jit(_take)/gather | solution.py:37
  750.2 15.4 %gather_fusion.39 = f32[4096,8]{1,0:T(8,128)} fusion(f32[8,6144]{0,1:T(8,128)S(1)} %copy.178, s32[4096]{0:T(1024)} %fusion.88), kind=kCustom, calls=%fused_computation.40.clone | custom fusion | bytes 278528 | tf_op jit(solution)/shard_map/jit(_take)/gather | solution.py:37
  765.7 15.4 %gather_fusion.38 = f32[4096,8]{1,0:T(8,128)} fusion(f32[8,6144]{0,1:T(8,128)S(1)} %copy.178, s32[4096]{0:T(1024)} %fusion.87), kind=kCustom, calls=%fused_computation.39.clone | custom fusion | bytes 278528 | tf_op jit(solution)/shard_map/jit(_take)/gather | solution.py:37
  781.1 15.4 %gather_fusion.37 = f32[4096,8]{1,0:T(8,128)} fusion(f32[8,6144]{0,1:T(8,128)S(1)} %copy.178, s32[4096]{0:T(1024)} %fusion.86), kind=kCustom, calls=%fused_computation.38.clone | custom fusion | bytes 278528 | tf_op jit(solution)/shard_map/jit(_take)/gather | solution.py:37
  796.5 15.4 %gather_fusion.36 = f32[4096,8]{1,0:T(8,128)} fusion(f32[8,6144]{0,1:T(8,128)S(1)} %copy.178, s32[4096]{0:T(1024)} %fusion.85), kind=kCustom, calls=%fused_computation.37.clone | custom fusion | bytes 278528 | tf_op jit(solution)/shard_map/jit(_take)/gather | solution.py:37
  826.0 6.4 gather_fusion.42
  833.8 10.4 all_to_all.39
  846.7 15.4 %gather_fusion.48 = f32[4096,8]{1,0:T(8,128)} fusion(f32[8,6144]{0,1:T(8,128)S(1)} %copy.192, s32[4096]{0:T(1024)} %fusion.90), kind=kCustom, calls=%fused_computation.48.clone | custom fusion | bytes 278528 | tf_op jit(solution)/shard_map/jit(_take)/gather | solution.py:37
  862.2 15.4 %gather_fusion.47 = f32[4096,8]{1,0:T(8,128)} fusion(f32[8,6144]{0,1:T(8,128)S(1)} %copy.192, s32[4096]{0:T(1024)} %fusion.89), kind=kCustom, calls=%fused_computation.47.clone | custom fusion | bytes 278528 | tf_op jit(solution)/shard_map/jit(_take)/gather | solution.py:37
  877.6 15.4 %gather_fusion.46 = f32[4096,8]{1,0:T(8,128)} fusion(f32[8,6144]{0,1:T(8,128)S(1)} %copy.192, s32[4096]{0:T(1024)} %fusion.88), kind=kCustom, calls=%fused_computation.46.clone | custom fusion | bytes 278528 | tf_op jit(solution)/shard_map/jit(_take)/gather | solution.py:37
  893.0 15.4 %gather_fusion.45 = f32[4096,8]{1,0:T(8,128)} fusion(f32[8,6144]{0,1:T(8,128)S(1)} %copy.192, s32[4096]{0:T(1024)} %fusion.87), kind=kCustom, calls=%fused_computation.45.clone | custom fusion | bytes 278528 | tf_op jit(solution)/shard_map/jit(_take)/gather | solution.py:37
  908.4 15.4 %gather_fusion.44 = f32[4096,8]{1,0:T(8,128)} fusion(f32[8,6144]{0,1:T(8,128)S(1)} %copy.192, s32[4096]{0:T(1024)} %fusion.86), kind=kCustom, calls=%fused_computation.44.clone | custom fusion | bytes 278528 | tf_op jit(solution)/shard_map/jit(_take)/gather | solution.py:37
  923.8 15.4 %gather_fusion.43 = f32[4096,8]{1,0:T(8,128)} fusion(f32[8,6144]{0,1:T(8,128)S(1)} %copy.192, s32[4096]{0:T(1024)} %fusion.85), kind=kCustom, calls=%fused_computation.43.clone | custom fusion | bytes 278528 | tf_op jit(solution)/shard_map/jit(_take)/gather | solution.py:37
  949.9 3.3 fusion.52
  954.5 92.4 %all-reduce.3.cloned.1.call-done = f32[128,4096]{1,0:T(8,128)} async-done(((f32[128,4096]{1,0:T(8,128)}), f32[128,4096]{1,0:T(8,128)}) %all-reduce.3.cloned.1.call-update) | async-done | bytes 2097168
  (382 shorter events, 134.6 us)
Async XLA Ops:
  6.5 943.2 %copy-start = (f32[128,128]{1,0:T(8,128)S(1)}, f32[128,128]{1,0:T(8,128)}, u32[]{:S(2)}) copy-start(f32[128,128]{1,0:T(8,128)} %param.13) | copy-start | bytes 196612
  6.5 56.2 %all-gather.2.cloned.1.call-start = ((), (), s32[]{:S(2)}) async-start(), calls=%async_computation.7 | async-start | bytes 2228224 | tf_op jit(solution)/shard_map/all_gather | solution.py:25
  11.1 54.3 %copy-start.115 = (f32[8]{0:T(128)}, f32[8]{0:T(128)S(1)}, u32[]{:S(2)}) copy-start(f32[8]{0:T(128)S(1)} %get-tuple-element.40) | copy-start | bytes 100
  65.4 130.4 %copy-start.19 = (f32[8,4096]{1,0:T(8,128)}, f32[8,4096]{1,0:T(8,128)S(1)}, u32[]{:S(2)}) copy-start(f32[8,4096]{1,0:T(8,128)S(1)} %get-tuple-element.42) | copy-start | bytes 393220
  72.5 10.5 copy-start.134
  72.5 10.5 copy-start.135
  72.5 10.5 copy-start.136
  74.5 16.3 %all-to-all-start = ((f32[8,16,128]{2,0,1:T(8,128)}), f32[8,16,128]{2,0,1:T(8,128)S(1)}, u32[]{:S(2)}, u32[]{:S(2)}) async-start(f32[8,16,128]{2,0,1:T(8,128)} %copy.107), calls=%async_computation | async-start | bytes 131072 | tf_op jit(solution)/shard_map/all_to_all | solution.py:31
  93.4 18.3 %copy-start.49 = (s32[4096]{0:T(1024)S(1)}, s32[4096]{0:T(1024)}, u32[]{:S(2)}) copy-start(s32[4096]{0:T(1024)} %fusion.89) | copy-start | bytes 49156
  111.6 16.9 %copy-start.47 = (s32[4096]{0:T(1024)S(1)}, s32[4096]{0:T(1024)}, u32[]{:S(2)}) copy-start(s32[4096]{0:T(1024)} %fusion.88) | copy-start | bytes 49156
  128.5 16.9 %copy-start.45 = (s32[4096]{0:T(1024)S(1)}, s32[4096]{0:T(1024)}, u32[]{:S(2)}) copy-start(s32[4096]{0:T(1024)} %fusion.87) | copy-start | bytes 49156
  145.4 16.9 %copy-start.41 = (s32[4096]{0:T(1024)S(1)}, s32[4096]{0:T(1024)}, u32[]{:S(2)}) copy-start(s32[4096]{0:T(1024)} %fusion.86) | copy-start | bytes 49156
  162.4 16.9 %copy-start.43 = (s32[4096]{0:T(1024)S(1)}, s32[4096]{0:T(1024)}, u32[]{:S(2)}) copy-start(s32[4096]{0:T(1024)} %fusion.85) | copy-start | bytes 49156
  205.3 13.1 %copy-start.51 = (s32[4096]{0:T(1024)S(1)}, s32[4096]{0:T(1024)}, u32[]{:S(2)}) copy-start(s32[4096]{0:T(1024)} %fusion.90) | copy-start | bytes 49156
  216.5 16.0 %copy-start.50 = (s32[4096]{0:T(1024)S(1)}, s32[4096]{0:T(1024)}, u32[]{:S(2)}) copy-start(s32[4096]{0:T(1024)} %fusion.89) | copy-start | bytes 49156
  216.5 30.1 %copy-start.48 = (s32[4096]{0:T(1024)S(1)}, s32[4096]{0:T(1024)}, u32[]{:S(2)}) copy-start(s32[4096]{0:T(1024)} %fusion.88) | copy-start | bytes 49156
  218.4 42.4 %copy-start.46 = (s32[4096]{0:T(1024)S(1)}, s32[4096]{0:T(1024)}, u32[]{:S(2)}) copy-start(s32[4096]{0:T(1024)} %fusion.87) | copy-start | bytes 49156
  218.4 56.4 %copy-start.42 = (s32[4096]{0:T(1024)S(1)}, s32[4096]{0:T(1024)}, u32[]{:S(2)}) copy-start(s32[4096]{0:T(1024)} %fusion.86) | copy-start | bytes 49156
  232.5 56.4 %copy-start.44 = (s32[4096]{0:T(1024)S(1)}, s32[4096]{0:T(1024)}, u32[]{:S(2)}) copy-start(s32[4096]{0:T(1024)} %fusion.85) | copy-start | bytes 49156
  303.0 4.5 copy-start.14
  308.1 4.6 copy-start.9
  321.3 5.6 copy-start.137
  323.2 11.4 %all-to-all-start.2 = ((f32[8,16,128]{2,0,1:T(8,128)}), f32[8,16,128]{2,0,1:T(8,128)S(1)}, u32[]{:S(2)}, u32[]{:S(2)}) async-start(f32[8,16,128]{2,0,1:T(8,128)} %copy.135), calls=%async_computation.2 | async-start | bytes 131072 | tf_op jit(solution)/shard_map/all_to_all | solution.py:31
  326.8 720.1 %all-reduce.3.cloned.1.call-start = ((), (), s32[]{:S(2)}) async-start(), calls=%async_computation.8 | async-start | bytes 4194304
  429.7 4.5 copy-start.15
  434.8 4.6 copy-start.10
  440.7 10.0 copy-start.106
  442.5 20.4 %copy-start.1 = (f32[8,4096]{1,0:T(8,128)}, f32[8,4096]{1,0:T(8,128)S(1)}, u32[]{:S(2)}) copy-start(f32[8,4096]{1,0:T(8,128)S(1)} %get-tuple-element.13) | copy-start | bytes 393220
  558.0 4.5 copy-start.16
  563.0 4.7 copy-start.11
  578.5 11.7 %copy-start.26 = (f32[8,4096]{1,0:T(8,128)S(1)}, f32[8,4096]{1,0:T(8,128)}, u32[]{:S(2)}) copy-start(f32[8,4096]{1,0:T(8,128)} %copy-done.25) | copy-start | bytes 393220
  685.2 4.5 copy-start.17
  690.3 4.6 copy-start.12
  695.5 9.2 copy-start.107
  696.5 20.4 %copy-start.4 = (f32[8,4096]{1,0:T(8,128)}, f32[8,4096]{1,0:T(8,128)S(1)}, u32[]{:S(2)}) copy-start(f32[8,4096]{1,0:T(8,128)S(1)} %get-tuple-element.9) | copy-start | bytes 393220
  811.9 4.5 copy-start.18
  817.0 4.7 copy-start.13
  819.3 3.6 copy-start.5
  819.3 3.6 copy-start.32
  819.3 3.6 copy-start.39
  819.3 3.6 copy-start.56
  819.3 3.6 copy-start.69
  819.3 3.6 copy-start.76
  819.3 3.6 copy-start.83
  832.4 11.8 %copy-start.24 = (f32[8,4096]{1,0:T(8,128)S(1)}, f32[8,4096]{1,0:T(8,128)}, u32[]{:S(2)}) copy-start(f32[8,4096]{1,0:T(8,128)} %copy-done.23) | copy-start | bytes 393220
  945.0 4.7 copy-start.3
  945.0 4.7 copy-start.6
  945.0 4.7 copy-start.20
  945.0 4.7 copy-start.22
  945.0 4.7 copy-start.33
  945.0 4.7 copy-start.40
  945.1 4.7 copy-start.54
  945.1 4.7 copy-start.70
  945.1 4.7 copy-start.77
  945.1 4.7 copy-start.84
  945.1 4.7 copy-start.91
  945.1 4.7 copy-start.98
  945.1 4.7 copy-start.105
  945.1 4.7 copy-start.114
  945.1 4.7 copy-start.119
  945.1 4.7 copy-start.122
  945.2 4.7 copy-start.125
  945.2 4.7 copy-start.131
  945.2 4.7 copy-start.133
  (79 other events, 235.9 us)
Sparse Core Ops, SparseCore 0:
  9.8 52.8 all-gather.1
  953.3 93.5 all-reduce.2
where the time goes:
time: 1070 us; the launch traced here: 1060 us
  local copies, waits for them, and re-layouts  788 us (74%)
  waiting for transfers between devices  149 us (14%)
  blocking collectives  52 us (5%)
  other arithmetic  32.2 us (3%)
  between operations  15.8 us (1%)
  starting transfers between devices  12.2 us (1%)
    gather x84, local copies, waits for them, and re-layouts, apply_operator(): jnp.take(extended, neighbours[slot_number], axis=1)  712 us
    unnamed x3, waiting for transfers between devices  93.1 us
    all_to_all x5, blocking collectives, apply_operator(): lax.all_to_all(outgoing.reshape(slab_rows, -1, HMAX), 'cells', split_axis...  52 us
    gather x7, local copies, waits for them, and re-layouts, apply_operator(): outgoing = jnp.take(field, send_cells, axis=1)  47.4 us
    all_gather x1, waiting for transfers between devices, local(): lax.all_gather(source_levels, 'lev', axis=0, tiled=True)  41.8 us
  transfers between devices with their start and end apart: 4, of which 4 were waited for; matrix products, arithmetic and copies ran while one was open for 1% of the time, Pallas kernels for 0%

commit v1 on v0

--- a/solution.py
+++ b/solution.py
@@ -1,3 +1,4 @@
+import functools
 import jax
 import jax.numpy as jnp
 from jax import lax
@@ -7,6 +8,18 @@
 HMAX = 128
 SWEEPS = 2
 STEPS = 4
+
+
+def search_desk_over_axis(array_here, dev_axis):
+    return jnp.concatenate(
+        lax.all_to_all(
+            jnp.stack([array_here for _ in range(lax.axis_size(dev_axis))]), dev_axis, 0, 0
+        ),
+        axis=0,
+    )
+
+
+attach_quotas_on = functools.partial(search_desk_over_axis, dev_axis="lev")
 
 
 def full_product(left, right):
@@ -22,7 +35,7 @@
     slot_total = send_cells.shape[0]
     diagonal = jnp.sum(edge_weight, axis=0)
     own_rows = lax.dynamic_slice_in_dim(level_to_mode, position * slab_rows, slab_rows, 0)
-    mode_field = full_product(own_rows, lax.all_gather(source_levels, "lev", axis=0, tiled=True))
+    mode_field = full_product(own_rows, attach_quotas_on(source_levels))
     shift_col = mode_shift[:, None]
     own_scale = shift_col + diagonal[None, :]
 

time: 1070 us -> 1020 us (0.953)
  local copies, waits for them, and re-layouts: 788 us -> 759 us
  waiting for transfers between devices: 149 us -> 128 us
  starting transfers between devices: 12.2 us -> 23.1 us
    all_gather x1 -> x0, waiting for transfers between devices: 41.8 us -> none  [local(): lax.all_gather(source_levels, 'lev', axis=0, tiled=True)]
    gather x84, local copies, waits for them, and re-layouts: 712 us -> 684 us  [apply_operator(): jnp.take(extended, neighbours[slot_number], axis=1)]
    all_to_all x0 -> x1, waiting for transfers between devices: none -> 22.2 us  [search_desk_over_axis(): lax.all_to_all(jnp.stack([array_here for _ in range(lax.axis_size(dev_axi...]
    unnamed x3 -> x2, waiting for transfers between devices: 93.1 us -> 91.2 us
where the time goes in v1:
time: 1020 us; the launch traced here: 1010 us
  local copies, waits for them, and re-layouts  759 us (74%)
  waiting for transfers between devices  128 us (13%)
  blocking collectives  52 us (5%)
  other arithmetic  27.3 us (3%)
  starting transfers between devices  23.1 us (2%)
  between operations  16.2 us (2%)
    gather x84, local copies, waits for them, and re-layouts, apply_operator(): jnp.take(extended, neighbours[slot_number], axis=1)  684 us
    unnamed x2, waiting for transfers between devices  91.2 us
    all_to_all x5, blocking collectives, apply_operator(): lax.all_to_all(outgoing.reshape(slab_rows, -1, HMAX), 'cells', split_axis...  52 us
    gather x7, local copies, waits for them, and re-layouts, apply_operator(): outgoing = jnp.take(field, send_cells, axis=1)  47.3 us
    all_to_all x1, waiting for transfers between devices, search_desk_over_axis(): lax.all_to_all(jnp.stack([array_here for _ in range(lax.axis_size(dev_axi...  22.2 us
  transfers between devices with their start and end apart: 4, of which 4 were waited for; matrix products, arithmetic and copies ran while one was open for 1% of the time, Pallas kernels for 0%

profile of v1, /device:TPU:1, one launch (start us, length us, event | category | flops | bytes accessed | tf_op | source)
XLA Modules:
  0.0 1010.5 jit_solution(3349470779411193542)
XLA Ops:
  9.0 7.7 all-to-all-start
  22.4 22.2 %all-to-all-done = f32[16,8,4096]{2,1,0:T(8,128)S(1)} async-done(((f32[16,8,4096]{2,1,0:T(8,128)}), f32[16,8,4096]{2,1,0:T(8,128)S(1)}, u32[]{:S(2)}, u32[]{:S(2)}) %all-to-all-start) | async-done | bytes 2097184 | tf_op jit(solution)/shard_map/all_to_all | solution.py:15
  47.0 6.4 gather_fusion
  55.4 11.9 %all-to-all-start.1 = ((f32[8,16,128]{2,0,1:T(8,128)}), f32[8,16,128]{2,0,1:T(8,128)S(1)}, u32[]{:S(2)}, u32[]{:S(2)}) async-start(f32[8,16,128]{2,0,1:T(8,128)} %copy.107), calls=%async_computation.1 | async-start | bytes 131072 | tf_op jit(solution)/shard_map/all_to_all | solution.py:44
  68.0 7.2 all-to-all-done.1
  77.7 15.4 %gather_fusion.6 = f32[4096,8]{1,0:T(8,128)} fusion(f32[8,6144]{0,1:T(8,128)S(1)} %copy.108, s32[4096]{0:T(1024)} %fusion.92), kind=kCustom, calls=%fused_computation.12.clone | custom fusion | bytes 278528 | tf_op jit(solution)/shard_map/jit(_take)/gather | solution.py:50
  93.1 2.8 copy.119
  95.9 14.1 %gather_fusion.5 = f32[4096,8]{1,0:T(8,128)} fusion(f32[8,6144]{0,1:T(8,128)S(1)} %copy.108, s32[4096]{0:T(1024)S(1)} %fusion.91), kind=kCustom, calls=%fused_computation.11.clone | custom fusion | bytes 278528 | tf_op jit(solution)/shard_map/jit(_take)/gather | solution.py:50
  112.8 14.1 %gather_fusion.4 = f32[4096,8]{1,0:T(8,128)} fusion(f32[8,6144]{0,1:T(8,128)S(1)} %copy.108, s32[4096]{0:T(1024)S(1)} %fusion.90), kind=kCustom, calls=%fused_computation.10.clone | custom fusion | bytes 278528 | tf_op jit(solution)/shard_map/jit(_take)/gather | solution.py:50
  126.9 2.8 copy.115
  129.7 14.1 %gather_fusion.3 = f32[4096,8]{1,0:T(8,128)} fusion(f32[8,6144]{0,1:T(8,128)S(1)} %copy.108, s32[4096]{0:T(1024)S(1)} %fusion.89), kind=kCustom, calls=%fused_computation.9.clone | custom fusion | bytes 278528 | tf_op jit(solution)/shard_map/jit(_take)/gather | solution.py:50
  146.6 14.1 %gather_fusion.2 = f32[4096,8]{1,0:T(8,128)} fusion(f32[8,6144]{0,1:T(8,128)S(1)} %copy.108, s32[4096]{0:T(1024)S(1)} %fusion.88), kind=kCustom, calls=%fused_computation.8.clone | custom fusion | bytes 278528 | tf_op jit(solution)/shard_map/jit(_take)/gather | solution.py:50
  163.5 14.1 %gather_fusion.1 = f32[4096,8]{1,0:T(8,128)} fusion(f32[8,6144]{0,1:T(8,128)S(1)} %copy.108, s32[4096]{0:T(1024)S(1)} %copy-done.70), kind=kCustom, calls=%fused_computation.1.clone | custom fusion | bytes 278528 | tf_op jit(solution)/shard_map/jit(_take)/gather | solution.py:50
  181.9 6.4 gather_fusion.7
  189.6 10.5 %all_to_all.40 = f32[8,16,128]{2,0,1:T(8,128)S(1)} all-to-all(f32[8,16,128]{2,0,1:T(8,128)S(1)} %copy.121), channel_id=1, replica_groups=mesh['cells'=16,'lev'=16] {'cells'}, dimensions={1} | all-to-all | bytes 131072 | tf_op jit(solution)/shard_map/all_to_all | solution.py:44
  202.7 14.1 %gather_fusion.13 = f32[4096,8]{1,0:T(8,128)} fusion(f32[8,6144]{0,1:T(8,128)S(1)} %copy.122, s32[4096]{0:T(1024)S(1)} %copy-done.27), kind=kCustom, calls=%fused_computation.18.clone | custom fusion | bytes 278528 | tf_op jit(solution)/shard_map/jit(_take)/gather | solution.py:50
  216.8 14.1 %gather_fusion.12 = f32[4096,8]{1,0:T(8,128)} fusion(f32[8,6144]{0,1:T(8,128)S(1)} %copy.122, s32[4096]{0:T(1024)S(1)} %fusion.91), kind=kCustom, calls=%fused_computation.17.clone | custom fusion | bytes 278528 | tf_op jit(solution)/shard_map/jit(_take)/gather | solution.py:50
  230.8 14.1 %gather_fusion.11 = f32[4096,8]{1,0:T(8,128)} fusion(f32[8,6144]{0,1:T(8,128)S(1)} %copy.122, s32[4096]{0:T(1024)S(1)} %fusion.90), kind=kCustom, calls=%fused_computation.16.clone | custom fusion | bytes 278528 | tf_op jit(solution)/shard_map/jit(_take)/gather | solution.py:50
  244.9 14.1 %gather_fusion.10 = f32[4096,8]{1,0:T(8,128)} fusion(f32[8,6144]{0,1:T(8,128)S(1)} %copy.122, s32[4096]{0:T(1024)S(1)} %fusion.89), kind=kCustom, calls=%fused_computation.15.clone | custom fusion | bytes 278528 | tf_op jit(solution)/shard_map/jit(_take)/gather | solution.py:50
  258.9 14.1 %gather_fusion.9 = f32[4096,8]{1,0:T(8,128)} fusion(f32[8,6144]{0,1:T(8,128)S(1)} %copy.122, s32[4096]{0:T(1024)S(1)} %fusion.88), kind=kCustom, calls=%fused_computation.14.clone | custom fusion | bytes 278528 | tf_op jit(solution)/shard_map/jit(_take)/gather | solution.py:50
  273.0 14.1 %gather_fusion.8 = f32[4096,8]{1,0:T(8,128)} fusion(f32[8,6144]{0,1:T(8,128)S(1)} %copy.122, s32[4096]{0:T(1024)S(1)} %copy-done.71), kind=kCustom, calls=%fused_computation.13.clone | custom fusion | bytes 278528 | tf_op jit(solution)/shard_map/jit(_take)/gather | solution.py:50
  299.0 6.4 gather_fusion.14
  307.3 3.4 all-to-all-start.3
  311.4 7.3 all-to-all-done.3
  321.2 15.4 %gather_fusion.20 = f32[4096,8]{1,0:T(8,128)} fusion(f32[8,6144]{0,1:T(8,128)S(1)} %copy.136, s32[4096]{0:T(1024)} %fusion.92), kind=kCustom, calls=%fused_computation.24.clone | custom fusion | bytes 278528 | tf_op jit(solution)/shard_map/jit(_take)/gather | solution.py:50
  336.6 14.1 %gather_fusion.19 = f32[4096,8]{1,0:T(8,128)} fusion(f32[8,6144]{0,1:T(8,128)S(1)} %copy.136, s32[4096]{0:T(1024)S(1)} %fusion.91), kind=kCustom, calls=%fused_computation.23.clone | custom fusion | bytes 278528 | tf_op jit(solution)/shard_map/jit(_take)/gather | solution.py:50
  350.6 14.1 %gather_fusion.18 = f32[4096,8]{1,0:T(8,128)} fusion(f32[8,6144]{0,1:T(8,128)S(1)} %copy.136, s32[4096]{0:T(1024)S(1)} %fusion.90), kind=kCustom, calls=%fused_computation.22.clone | custom fusion | bytes 278528 | tf_op jit(solution)/shard_map/jit(_take)/gather | solution.py:50
  364.7 14.1 %gather_fusion.17 = f32[4096,8]{1,0:T(8,128)} fusion(f32[8,6144]{0,1:T(8,128)S(1)} %copy.136, s32[4096]{0:T(1024)S(1)} %fusion.89), kind=kCustom, calls=%fused_computation.21.clone | custom fusion | bytes 278528 | tf_op jit(solution)/shard_map/jit(_take)/gather | solution.py:50
  378.8 14.1 %gather_fusion.16 = f32[4096,8]{1,0:T(8,128)} fusion(f32[8,6144]{0,1:T(8,128)S(1)} %copy.136, s32[4096]{0:T(1024)S(1)} %fusion.88), kind=kCustom, calls=%fused_computation.20.clone | custom fusion | bytes 278528 | tf_op jit(solution)/shard_map/jit(_take)/gather | solution.py:50
  392.8 15.4 %gather_fusion.15 = f32[4096,8]{1,0:T(8,128)} fusion(f32[8,6144]{0,1:T(8,128)S(1)} %copy.136, s32[4096]{0:T(1024)} %fusion.87), kind=kCustom, calls=%fused_computation.19.clone | custom fusion | bytes 278528 | tf_op jit(solution)/shard_map/jit(_take)/gather | solution.py:50
  421.7 7.6 gather_fusion.21
  431.2 10.4 %all_to_all.41 = f32[8,16,128]{2,0,1:T(8,128)S(1)} all-to-all(f32[8,16,128]{2,0,1:T(8,128)S(1)} %copy.149), channel_id=1, replica_groups=mesh['cells'=16,'lev'=16] {'cells'}, dimensions={1} | all-to-all | bytes 131072 | tf_op jit(solution)/shard_map/all_to_all | solution.py:44
  444.1 15.4 %gather_fusion.27 = f32[4096,8]{1,0:T(8,128)} fusion(f32[8,6144]{0,1:T(8,128)S(1)} %copy.150, s32[4096]{0:T(1024)} %fusion.92), kind=kCustom, calls=%fused_computation.30.clone | custom fusion | bytes 278528 | tf_op jit(solution)/shard_map/jit(_take)/gather | solution.py:50
  459.5 14.1 %gather_fusion.26 = f32[4096,8]{1,0:T(8,128)} fusion(f32[8,6144]{0,1:T(8,128)S(1)} %copy.150, s32[4096]{0:T(1024)S(1)} %fusion.91), kind=kCustom, calls=%fused_computation.29.clone | custom fusion | bytes 278528 | tf_op jit(solution)/shard_map/jit(_take)/gather | solution.py:50
  473.6 14.1 %gather_fusion.25 = f32[4096,8]{1,0:T(8,128)} fusion(f32[8,6144]{0,1:T(8,128)S(1)} %copy.150, s32[4096]{0:T(1024)S(1)} %fusion.90), kind=kCustom, calls=%fused_computation.28.clone | custom fusion | bytes 278528 | tf_op jit(solution)/shard_map/jit(_take)/gather | solution.py:50
  487.6 14.1 %gather_fusion.24 = f32[4096,8]{1,0:T(8,128)} fusion(f32[8,6144]{0,1:T(8,128)S(1)} %copy.150, s32[4096]{0:T(1024)S(1)} %fusion.89), kind=kCustom, calls=%fused_computation.27.clone | custom fusion | bytes 278528 | tf_op jit(solution)/shard_map/jit(_take)/gather | solution.py:50
  501.7 14.1 %gather_fusion.23 = f32[4096,8]{1,0:T(8,128)} fusion(f32[8,6144]{0,1:T(8,128)S(1)} %copy.150, s32[4096]{0:T(1024)S(1)} %fusion.88), kind=kCustom, calls=%fused_computation.26.clone | custom fusion | bytes 278528 | tf_op jit(solution)/shard_map/jit(_take)/gather | solution.py:50
  515.8 15.4 %gather_fusion.22 = f32[4096,8]{1,0:T(8,128)} fusion(f32[8,6144]{0,1:T(8,128)S(1)} %copy.150, s32[4096]{0:T(1024)} %fusion.87), kind=kCustom, calls=%fused_computation.25.clone | custom fusion | bytes 278528 | tf_op jit(solution)/shard_map/jit(_take)/gather | solution.py:50
  545.3 6.4 gather_fusion.28
  553.1 10.3 %all_to_all.42 = f32[8,16,128]{2,0,1:T(8,128)S(1)} all-to-all(f32[8,16,128]{2,0,1:T(8,128)S(1)} %copy.163), channel_id=1, replica_groups=mesh['cells'=16,'lev'=16] {'cells'}, dimensions={1} | all-to-all | bytes 131072 | tf_op jit(solution)/shard_map/all_to_all | solution.py:44
  565.9 15.4 %gather_fusion.34 = f32[4096,8]{1,0:T(8,128)} fusion(f32[8,6144]{0,1:T(8,128)S(1)} %copy.164, s32[4096]{0:T(1024)} %fusion.92), kind=kCustom, calls=%fused_computation.36.clone | custom fusion | bytes 278528 | tf_op jit(solution)/shard_map/jit(_take)/gather | solution.py:50
  581.4 14.1 %gather_fusion.33 = f32[4096,8]{1,0:T(8,128)} fusion(f32[8,6144]{0,1:T(8,128)S(1)} %copy.164, s32[4096]{0:T(1024)S(1)} %fusion.91), kind=kCustom, calls=%fused_computation.35.clone | custom fusion | bytes 278528 | tf_op jit(solution)/shard_map/jit(_take)/gather | solution.py:50
  595.4 14.1 %gather_fusion.32 = f32[4096,8]{1,0:T(8,128)} fusion(f32[8,6144]{0,1:T(8,128)S(1)} %copy.164, s32[4096]{0:T(1024)S(1)} %fusion.90), kind=kCustom, calls=%fused_computation.34.clone | custom fusion | bytes 278528 | tf_op jit(solution)/shard_map/jit(_take)/gather | solution.py:50
  609.5 14.1 %gather_fusion.31 = f32[4096,8]{1,0:T(8,128)} fusion(f32[8,6144]{0,1:T(8,128)S(1)} %copy.164, s32[4096]{0:T(1024)S(1)} %fusion.89), kind=kCustom, calls=%fused_computation.33.clone | custom fusion | bytes 278528 | tf_op jit(solution)/shard_map/jit(_take)/gather | solution.py:50
  623.5 14.1 %gather_fusion.30 = f32[4096,8]{1,0:T(8,128)} fusion(f32[8,6144]{0,1:T(8,128)S(1)} %copy.164, s32[4096]{0:T(1024)S(1)} %fusion.88), kind=kCustom, calls=%fused_computation.32.clone | custom fusion | bytes 278528 | tf_op jit(solution)/shard_map/jit(_take)/gather | solution.py:50
  637.6 15.4 %gather_fusion.29 = f32[4096,8]{1,0:T(8,128)} fusion(f32[8,6144]{0,1:T(8,128)S(1)} %copy.164, s32[4096]{0:T(1024)} %fusion.87), kind=kCustom, calls=%fused_computation.31.clone | custom fusion | bytes 278528 | tf_op jit(solution)/shard_map/jit(_take)/gather | solution.py:50
  665.6 7.6 gather_fusion.35
  675.0 10.4 %all_to_all.43 = f32[8,16,128]{2,0,1:T(8,128)S(1)} all-to-all(f32[8,16,128]{2,0,1:T(8,128)S(1)} %copy.177), channel_id=1, replica_groups=mesh['cells'=16,'lev'=16] {'cells'}, dimensions={1} | all-to-all | bytes 131072 | tf_op jit(solution)/shard_map/all_to_all | solution.py:44
  688.0 15.4 %gather_fusion.41 = f32[4096,8]{1,0:T(8,128)} fusion(f32[8,6144]{0,1:T(8,128)S(1)} %copy.178, s32[4096]{0:T(1024)} %fusion.92), kind=kCustom, calls=%fused_computation.42.clone | custom fusion | bytes 278528 | tf_op jit(solution)/shard_map/jit(_take)/gather | solution.py:50
  703.4 14.1 %gather_fusion.40 = f32[4096,8]{1,0:T(8,128)} fusion(f32[8,6144]{0,1:T(8,128)S(1)} %copy.178, s32[4096]{0:T(1024)S(1)} %fusion.91), kind=kCustom, calls=%fused_computation.41.clone | custom fusion | bytes 278528 | tf_op jit(solution)/shard_map/jit(_take)/gather | solution.py:50
  717.4 14.1 %gather_fusion.39 = f32[4096,8]{1,0:T(8,128)} fusion(f32[8,6144]{0,1:T(8,128)S(1)} %copy.178, s32[4096]{0:T(1024)S(1)} %fusion.90), kind=kCustom, calls=%fused_computation.40.clone | custom fusion | bytes 278528 | tf_op jit(solution)/shard_map/jit(_take)/gather | solution.py:50
  731.5 14.1 %gather_fusion.38 = f32[4096,8]{1,0:T(8,128)} fusion(f32[8,6144]{0,1:T(8,128)S(1)} %copy.178, s32[4096]{0:T(1024)S(1)} %fusion.89), kind=kCustom, calls=%fused_computation.39.clone | custom fusion | bytes 278528 | tf_op jit(solution)/shard_map/jit(_take)/gather | solution.py:50
  745.6 14.1 %gather_fusion.37 = f32[4096,8]{1,0:T(8,128)} fusion(f32[8,6144]{0,1:T(8,128)S(1)} %copy.178, s32[4096]{0:T(1024)S(1)} %fusion.88), kind=kCustom, calls=%fused_computation.38.clone | custom fusion | bytes 278528 | tf_op jit(solution)/shard_map/jit(_take)/gather | solution.py:50
  759.6 15.4 %gather_fusion.36 = f32[4096,8]{1,0:T(8,128)} fusion(f32[8,6144]{0,1:T(8,128)S(1)} %copy.178, s32[4096]{0:T(1024)} %fusion.87), kind=kCustom, calls=%fused_computation.37.clone | custom fusion | bytes 278528 | tf_op jit(solution)/shard_map/jit(_take)/gather | solution.py:50
  789.2 6.4 gather_fusion.42
  796.9 10.4 %all_to_all.44 = f32[8,16,128]{2,0,1:T(8,128)S(1)} all-to-all(f32[8,16,128]{2,0,1:T(8,128)S(1)} %copy.191), channel_id=1, replica_groups=mesh['cells'=16,'lev'=16] {'cells'}, dimensions={1} | all-to-all | bytes 131072 | tf_op jit(solution)/shard_map/all_to_all | solution.py:44
  809.8 15.4 %gather_fusion.48 = f32[4096,8]{1,0:T(8,128)} fusion(f32[8,6144]{0,1:T(8,128)S(1)} %copy.192, s32[4096]{0:T(1024)} %fusion.92), kind=kCustom, calls=%fused_computation.48.clone | custom fusion | bytes 278528 | tf_op jit(solution)/shard_map/jit(_take)/gather | solution.py:50
  825.3 14.1 %gather_fusion.47 = f32[4096,8]{1,0:T(8,128)} fusion(f32[8,6144]{0,1:T(8,128)S(1)} %copy.192, s32[4096]{0:T(1024)S(1)} %fusion.91), kind=kCustom, calls=%fused_computation.47.clone | custom fusion | bytes 278528 | tf_op jit(solution)/shard_map/jit(_take)/gather | solution.py:50
  839.3 14.1 %gather_fusion.46 = f32[4096,8]{1,0:T(8,128)} fusion(f32[8,6144]{0,1:T(8,128)S(1)} %copy.192, s32[4096]{0:T(1024)S(1)} %fusion.90), kind=kCustom, calls=%fused_computation.46.clone | custom fusion | bytes 278528 | tf_op jit(solution)/shard_map/jit(_take)/gather | solution.py:50
  853.4 14.1 %gather_fusion.45 = f32[4096,8]{1,0:T(8,128)} fusion(f32[8,6144]{0,1:T(8,128)S(1)} %copy.192, s32[4096]{0:T(1024)S(1)} %fusion.89), kind=kCustom, calls=%fused_computation.45.clone | custom fusion | bytes 278528 | tf_op jit(solution)/shard_map/jit(_take)/gather | solution.py:50
  867.4 14.1 %gather_fusion.44 = f32[4096,8]{1,0:T(8,128)} fusion(f32[8,6144]{0,1:T(8,128)S(1)} %copy.192, s32[4096]{0:T(1024)S(1)} %fusion.88), kind=kCustom, calls=%fused_computation.44.clone | custom fusion | bytes 278528 | tf_op jit(solution)/shard_map/jit(_take)/gather | solution.py:50
  881.5 14.1 %gather_fusion.43 = f32[4096,8]{1,0:T(8,128)} fusion(f32[8,6144]{0,1:T(8,128)S(1)} %copy.192, s32[4096]{0:T(1024)S(1)} %copy-done.72), kind=kCustom, calls=%fused_computation.43.clone | custom fusion | bytes 278528 | tf_op jit(solution)/shard_map/jit(_take)/gather | solution.py:50
  906.4 3.3 fusion.54
  910.9 91.1 %all-reduce.3.cloned.1.call-done = f32[128,4096]{1,0:T(8,128)} async-done(((f32[128,4096]{1,0:T(8,128)}), f32[128,4096]{1,0:T(8,128)}) %all-reduce.3.cloned.1.call-update) | async-done | bytes 2097168
  (420 shorter events, 130.9 us)
Async XLA Ops:
  6.5 899.6 %copy-start = (f32[128,128]{1,0:T(8,128)S(1)}, f32[128,128]{1,0:T(8,128)}, u32[]{:S(2)}) copy-start(f32[128,128]{1,0:T(8,128)} %param.13) | copy-start | bytes 196612
  9.0 7.8 copy-start.137
  9.0 8.9 copy-start.129
  9.0 9.6 copy-start.85
  9.0 9.7 copy-start.130
  9.0 35.6 %all-to-all-start = ((f32[16,8,4096]{2,1,0:T(8,128)}), f32[16,8,4096]{2,1,0:T(8,128)S(1)}, u32[]{:S(2)}, u32[]{:S(2)}) async-start(f32[16,8,4096]{2,1,0:T(8,128)} %stack.2), calls=%async_computation | async-start | bytes 4194304 | tf_op jit(solution)/shard_map/all_to_all | solution.py:15
  19.3 27.1 %copy-start.138 = (f32[8]{0:T(128)}, f32[8]{0:T(128)S(1)}, u32[]{:S(2)}) copy-start(f32[8]{0:T(128)S(1)} %get-tuple-element.40) | copy-start | bytes 100
  46.4 133.8 %copy-start.19 = (f32[8,4096]{1,0:T(8,128)}, f32[8,4096]{1,0:T(8,128)S(1)}, u32[]{:S(2)}) copy-start(f32[8,4096]{1,0:T(8,128)S(1)} %get-tuple-element.42) | copy-start | bytes 393220
  53.5 13.9 %copy-start.153 = (f32[8]{0:T(128)S(1)}, f32[8]{0:T(128)}, u32[]{:S(2)}) copy-start(f32[8]{0:T(128)} %get-tuple-element.17) | copy-start | bytes 100
  53.5 13.9 %copy-start.154 = (f32[8]{0:T(128)S(1)}, f32[8]{0:T(128)}, u32[]{:S(2)}) copy-start(f32[8]{0:T(128)} %get-tuple-element.18) | copy-start | bytes 100
  53.5 13.9 %copy-start.155 = (f32[8]{0:T(128)S(1)}, f32[8]{0:T(128)}, u32[]{:S(2)}) copy-start(f32[8]{0:T(128)} %get-tuple-element.19) | copy-start | bytes 100
  55.4 19.7 %all-to-all-start.1 = ((f32[8,16,128]{2,0,1:T(8,128)}), f32[8,16,128]{2,0,1:T(8,128)S(1)}, u32[]{:S(2)}, u32[]{:S(2)}) async-start(f32[8,16,128]{2,0,1:T(8,128)} %copy.107), calls=%async_computation.1 | async-start | bytes 131072 | tf_op jit(solution)/shard_map/all_to_all | solution.py:44
  146.6 16.9 %copy-start.70 = (s32[4096]{0:T(1024)S(1)}, s32[4096]{0:T(1024)}, u32[]{:S(2)}) copy-start(s32[4096]{0:T(1024)} %fusion.87) | copy-start | bytes 49156
  189.6 13.1 %copy-start.27 = (s32[4096]{0:T(1024)S(1)}, s32[4096]{0:T(1024)}, u32[]{:S(2)}) copy-start(s32[4096]{0:T(1024)} %fusion.92) | copy-start | bytes 49156
  216.8 56.2 %copy-start.71 = (s32[4096]{0:T(1024)S(1)}, s32[4096]{0:T(1024)}, u32[]{:S(2)}) copy-start(s32[4096]{0:T(1024)} %fusion.87) | copy-start | bytes 49156
  287.1 4.5 copy-start.14
  292.1 4.7 copy-start.9
  305.5 5.4 copy-start.156
  307.3 11.3 %all-to-all-start.3 = ((f32[8,16,128]{2,0,1:T(8,128)}), f32[8,16,128]{2,0,1:T(8,128)S(1)}, u32[]{:S(2)}, u32[]{:S(2)}) async-start(f32[8,16,128]{2,0,1:T(8,128)} %copy.135), calls=%async_computation.3 | async-start | bytes 131072 | tf_op jit(solution)/shard_map/all_to_all | solution.py:44
  310.8 691.3 %all-reduce.3.cloned.1.call-start = ((), (), s32[]{:S(2)}) async-start(), calls=%async_computation.8 | async-start | bytes 4194304
  408.2 4.5 copy-start.15
  413.3 4.7 copy-start.10
  419.3 10.0 copy-start.128
  421.1 20.4 %copy-start.1 = (f32[8,4096]{1,0:T(8,128)}, f32[8,4096]{1,0:T(8,128)S(1)}, u32[]{:S(2)}) copy-start(f32[8,4096]{1,0:T(8,128)S(1)} %get-tuple-element.13) | copy-start | bytes 393220
  531.2 4.5 copy-start.16
  536.2 4.7 copy-start.11
  538.5 3.7 copy-start.31
  538.5 3.7 copy-start.38
  538.5 3.7 copy-start.45
  551.8 11.6 %copy-start.26 = (f32[8,4096]{1,0:T(8,128)S(1)}, f32[8,4096]{1,0:T(8,128)}, u32[]{:S(2)}) copy-start(f32[8,4096]{1,0:T(8,128)} %copy-done.25) | copy-start | bytes 393220
  653.0 4.5 copy-start.17
  658.1 4.7 copy-start.12
  665.0 20.4 %copy-start.4 = (f32[8,4096]{1,0:T(8,128)}, f32[8,4096]{1,0:T(8,128)S(1)}, u32[]{:S(2)}) copy-start(f32[8,4096]{1,0:T(8,128)S(1)} %get-tuple-element.9) | copy-start | bytes 393220
  775.0 4.5 copy-start.18
  780.1 4.7 copy-start.13
  782.4 3.7 copy-start.5
  782.4 3.7 copy-start.33
  782.4 3.7 copy-start.40
  782.4 3.7 copy-start.47
  795.6 11.7 %copy-start.24 = (f32[8,4096]{1,0:T(8,128)S(1)}, f32[8,4096]{1,0:T(8,128)}, u32[]{:S(2)}) copy-start(f32[8,4096]{1,0:T(8,128)} %copy-done.23) | copy-start | bytes 393220
  839.3 42.2 %copy-start.72 = (s32[4096]{0:T(1024)S(1)}, s32[4096]{0:T(1024)}, u32[]{:S(2)}) copy-start(s32[4096]{0:T(1024)} %fusion.87) | copy-start | bytes 49156
  901.4 4.7 copy-start.3
  901.4 4.8 copy-start.6
  901.4 4.8 copy-start.20
  901.4 4.8 copy-start.22
  901.4 4.8 copy-start.34
  901.4 4.8 copy-start.41
  901.4 4.8 copy-start.48
  901.4 4.8 copy-start.55
  901.4 4.8 copy-start.62
  901.4 4.8 copy-start.69
  901.4 4.8 copy-start.75
  901.5 4.8 copy-start.92
  901.5 4.8 copy-start.99
  901.5 4.8 copy-start.106
  901.5 4.8 copy-start.113
  901.5 4.8 copy-start.120
  901.5 4.8 copy-start.127
  901.5 4.8 copy-start.136
  901.5 4.8 copy-start.141
  901.5 4.8 copy-start.144
  901.6 4.8 copy-start.146
  901.6 4.8 copy-start.150
  901.6 4.8 copy-start.152
  (98 other events, 303.0 us)
Sparse Core Ops, SparseCore 0:
  909.8 92.2 all-reduce.2
